TPU v7x, 32 devices: a whole 2x2x4 slice. The times are simulated.
32 devices in a mesh: dp: 16 (over z, x, core), section: 2 (over y).
Axes of the slice: x: 2, y: 2, z: 4, core: 2. Of those that a mesh axis runs over, the one named last changes fastest.
Arguments:
- section_inputs: bfloat16 [2, 128, 8, 4, 4, 768], P('section', 'dp'), may hold values from -6 to 6
- cotangent: bfloat16 [128, 8, 4, 4, 128], P('dp'), may hold values from -6 to 6
- sessions: int32 [128], P('dp'), may hold values from 0 to 3
- point_weight: bfloat16 [2, 768, 768], P('section', 'dp'), may hold values from -0.21875 to 0.21875
- spatial_kernel: float32 [2, 9, 768], P('section'), may hold values from -1.5 to 1.5
- temporal_kernel: float32 [2, 5, 768], P('section'), may hold values from -2 to 2
- readout: bfloat16 [4, 128, 768], replicated, may hold values from -0.5 to 0.5
Outputs:
- point_grads: float32 [2, 768, 768], P('section', 'dp')
- spatial_grads: float32 [2, 9, 768], P('section')
- temporal_grads: float32 [2, 5, 768], P('section')
All inputs are finite; a program needn't handle non-finite values.
Results may differ from a plain program's by a relative error of at most 0.0071.
Values may be sent and summed in bfloat16 or wider, within the bound.
A program may use at most 64 MiB of HBM per device.

v0:
```python
import math
import jax
import jax.numpy as jnp
from jax import lax
from jax.sharding import PartitionSpec as P

INV_ROOT_TWO = 0.7071067811865476
INV_ROOT_TAU = 0.3989422804014327


def from_behind(block, axis, distance):
    devices = range(lax.axis_size(axis))
    route = [(i - distance, i) for i in devices if i - distance in devices]
    return lax.ppermute(block, axis, route)


def gelu_value(pre_act):
    return 0.5 * pre_act * (1.0 + jax.scipy.special.erf(pre_act * INV_ROOT_TWO))


def gelu_slope(pre_act):
    return (
        0.5 * (1.0 + jax.scipy.special.erf(pre_act * INV_ROOT_TWO))
        + pre_act * jnp.exp(-0.5 * pre_act * pre_act) * INV_ROOT_TAU
    )


def spatial_pad(field_in):
    pad_spec = [(0, 0)] * (field_in.ndim - 3) + [(1, 1), (1, 1), (0, 0)]
    return jnp.pad(field_in, pad_spec)


def spatial(field_in, kernel):
    height, width = (field_in.shape[-3], field_in.shape[-2])
    padded = spatial_pad(field_in)
    summed = jnp.zeros_like(field_in)
    for row_off in range(3):
        for col_off in range(3):
            summed = (
                summed
                + kernel[3 * row_off + col_off]
                * padded[..., row_off : row_off + height, col_off : col_off + width, :]
            )
    return summed


def spatial_back(grad_in, kernel):
    height, width = (grad_in.shape[-3], grad_in.shape[-2])
    padded = spatial_pad(grad_in)
    summed = jnp.zeros_like(grad_in)
    for row_off in range(3):
        for col_off in range(3):
            summed = (
                summed
                + kernel[3 * row_off + col_off]
                * padded[
                    ..., 2 - row_off : 2 - row_off + height, 2 - col_off : 2 - col_off + width, :
                ]
            )
    return summed


def spatial_kernel_grad(field_in, grad_in):
    height, width = (field_in.shape[-3], field_in.shape[-2])
    padded = spatial_pad(field_in)
    axes_all = tuple(range(field_in.ndim - 1))
    parts = []
    for row_off in range(3):
        for col_off in range(3):
            parts.append(
                jnp.sum(
                    padded[..., row_off : row_off + height, col_off : col_off + width, :] * grad_in,
                    axis=axes_all,
                )
            )
    return jnp.stack(parts)


def front_pad(field_in, tap_count):
    pad_spec = [(0, 0)] * (field_in.ndim - 4) + [(tap_count - 1, 0), (0, 0), (0, 0), (0, 0)]
    return jnp.pad(field_in, pad_spec)


def temporal(field_in, kernel):
    tap_count = kernel.shape[0]
    frames = field_in.shape[-4]
    padded = front_pad(field_in, tap_count)
    summed = jnp.zeros_like(field_in)
    for delay in range(tap_count):
        first = tap_count - 1 - delay
        summed = summed + kernel[delay] * padded[..., first : first + frames, :, :, :]
    return summed


def temporal_back(grad_in, kernel):
    tap_count = kernel.shape[0]
    frames = grad_in.shape[-4]
    pad_spec = [(0, 0)] * (grad_in.ndim - 4) + [(0, tap_count - 1), (0, 0), (0, 0), (0, 0)]
    padded = jnp.pad(grad_in, pad_spec)
    summed = jnp.zeros_like(grad_in)
    for delay in range(tap_count):
        summed = summed + kernel[delay] * padded[..., delay : delay + frames, :, :, :]
    return summed


def temporal_kernel_grad(field_in, grad_in, tap_count):
    frames = field_in.shape[-4]
    padded = front_pad(field_in, tap_count)
    axes_all = tuple(range(field_in.ndim - 1))
    parts = []
    for delay in range(tap_count):
        first = tap_count - 1 - delay
        parts.append(jnp.sum(padded[..., first : first + frames, :, :, :] * grad_in, axis=axes_all))
    return jnp.stack(parts)


def section_back(inputs, grad_out, s_kernel, t_kernel, hidden_of):
    field_in = inputs.astype(jnp.float32)
    spread = spatial(field_in, s_kernel)
    pre_act = temporal(spread, t_kernel)
    hidden = gelu_value(pre_act).astype(jnp.bfloat16)
    channels = inputs.shape[-1]
    flat_grad = grad_out.reshape(-1, channels)
    flat_hidden = hidden.reshape(-1, channels)
    hidden_grad = hidden_of(flat_grad).reshape(pre_act.shape)
    pre_grad = hidden_grad * gelu_slope(pre_act)
    spread_grad = temporal_back(pre_grad, t_kernel)
    in_grad = (grad_out.astype(jnp.float32) + spatial_back(spread_grad, s_kernel)).astype(
        jnp.bfloat16
    )
    weight_grad = jnp.dot(flat_hidden.T, flat_grad, preferred_element_type=jnp.float32)
    s_part = spatial_kernel_grad(field_in, spread_grad)
    t_part = temporal_kernel_grad(spread, pre_grad, t_kernel.shape[0])
    return (in_grad, weight_grad, s_part, t_part)


def local(
    section_inputs, cotangent, sessions, point_weight, spatial_kernel, temporal_kernel, readout
):
    section_count = lax.axis_size("section")
    my_section = lax.axis_index("section")
    inputs = section_inputs[0]
    s_kernel = spatial_kernel[0]
    t_kernel = temporal_kernel[0]
    weight_shard = point_weight[0]
    clip_count = inputs.shape[0]
    channels = inputs.shape[-1]
    chosen = jnp.take(readout, sessions, axis=0)
    top_grads = jnp.einsum(
        "cfhwr,crk->cfhwk", cotangent, chosen, preferred_element_type=jnp.float32
    ).astype(jnp.bfloat16)
    block_size = 2
    step_count = clip_count // block_size
    tick_count = step_count + section_count - 1
    full_weight = lax.all_gather(weight_shard, "dp", axis=0, tiled=True)

    def hidden_of(flat_grad):
        return jnp.dot(flat_grad, full_weight.T, preferred_element_type=jnp.float32)

    block_shape = (block_size,) + inputs.shape[1:]

    def tick(tick_index, state_now):
        incoming, w_sum, s_sum, t_sum = state_now
        clip_step = tick_index - (section_count - 1 - my_section)
        is_live = (clip_step >= 0) & (clip_step < step_count)
        first_clip = jnp.clip(clip_step, 0, step_count - 1) * block_size
        inputs_block = lax.dynamic_slice_in_dim(inputs, first_clip, block_size, 0)
        top_block = lax.dynamic_slice_in_dim(top_grads, first_clip, block_size, 0)
        grad_out = jnp.where(my_section == section_count - 1, top_block, incoming)

        def live_work(sums):
            in_grad, w_part, s_part, t_part = section_back(
                inputs_block, grad_out, s_kernel, t_kernel, hidden_of
            )
            return (in_grad, sums[0] + w_part, sums[1] + s_part, sums[2] + t_part)

        def dead_work(sums):
            return (jnp.zeros(block_shape, jnp.bfloat16), sums[0], sums[1], sums[2])

        in_grad, w_new, s_new, t_new = lax.cond(
            is_live, live_work, dead_work, (w_sum, s_sum, t_sum)
        )
        passed = from_behind(in_grad, "section", -1)
        return (passed, w_new, s_new, t_new)

    start_state = (
        jnp.zeros(block_shape, jnp.bfloat16),
        jnp.zeros((channels, channels), jnp.float32),
        jnp.zeros((9, channels), jnp.float32),
        jnp.zeros(t_kernel.shape, jnp.float32),
    )
    finals = lax.fori_loop(0, tick_count, tick, start_state)
    weight_grads = lax.psum_scatter(finals[1], "dp", scatter_dimension=0, tiled=True)
    s_total, t_total = lax.psum((finals[2], finals[3]), "dp")
    rows_all = (
        clip_count * lax.axis_size("dp") * inputs.shape[1] * inputs.shape[2] * inputs.shape[3]
    )
    factor = 1.0 / math.sqrt(rows_all)
    return ((weight_grads * factor)[None], (s_total * factor)[None], (t_total * factor)[None])


def solution(mesh):
    return jax.shard_map(
        local,
        mesh=mesh,
        in_specs=(
            P("section", "dp", None, None, None, None),
            P("dp", None, None, None, None),
            P("dp"),
            P("section", "dp", None),
            P("section", None, None),
            P("section", None, None),
            P(),
        ),
        out_specs=(P("section", "dp", None), P("section", None, None), P("section", None, None)),
        check_vma=False,
    )
```

profile of v0, /device:TPU:0, one launch (start us, length us, event | category | flops | bytes accessed | tf_op | source)
XLA Modules:
  0.0 254.5 jit_solution(1457571173146096510)
XLA Ops:
  7.2 0.7 all-gather.3.cloned.1.call-update
  8.0 1.3 copy.24
  9.3 1.4 copy.23
  10.7 3.1 %copy.22 = bf16[1,8,8,4,4,768]{5,2,4,3,1,0:T(8,128)(2,1)} copy(bf16[1,8,8,4,4,768]{5,4,3,2,1,0:T(4,128)(2,1)} %param.11) | data formatting | bytes 3145728 | tf_op args[0]
  13.8 0.6 gather_fusion
  14.7 1.8 fusion.36
  16.5 34.8 %all-gather.3.cloned.1.call-done = bf16[1,768,768]{2,1,0:T(8,128)(2,1)} async-done(((bf16[1,48,768]{2,1,0:T(8,128)(2,1)}), bf16[1,768,768]{2,1,0:T(8,128)(2,1)}) %all-gather.3.cloned.1.call-update) | async-done | bytes 1179664 | tf_op jit(solution)/shard_map/all_gather | solution.py:155
  51.4 0.6 broadcast_in_dim.32
  52.0 0.6 broadcast_in_dim.31
  52.6 1.6 broadcast_in_dim.30
  54.2 130.3 %while.21 = (s32[]{:T(128)}, bf16[2,8,4,4,768]{4,1,3,2,0:T(8,128)(2,1)S(1)}, f32[768,768]{1,0:T(8,128)}, f32[9,768]{1,0:T(8,128)}, f32[5,768]{1,0:T(8,128)}, /*i...) while((s32[]{:T(128)}, ...), condition=%wide.region_17.18_spmd, body=%wide.region_0.17_spmd.sunk | while | flops 625999872 | bytes 24124888 | solution.py:192
  54.2 1.3 collective-permute-start
  55.5 25.5 %collective-permute-done = bf16[2,8,4,4,768]{4,1,3,2,0:T(8,128)(2,1)S(1)} collective-permute-done((bf16[2,8,4,4,768]{4,1,3,2,0:T(8,128)(2,1)S(1)}, bf16[2,8,4,4,768]{4,1,3,2,0:T(8,128)(2,1)S(1)}, u32[]{:S(2)}, u32[]{:S(2)}) %collective-permute-start) | collective-permute-done | bytes 393248 | tf_op jit(solution)/shard_map/while/body/eval_jaxpr/ppermute | solution.py:14
  81.0 14.6 %conditional.2 = (bf16[2,8,4,4,768]{4,1,3,2,0:T(8,128)(2,1)S(1)}, f32[768,768]{1,0:T(8,128)}, f32[9,768]{1,0:T(8,128)}, f32[5,768]{1,0:T(8,128)}) conditional(s32[]{:T(128)} %convert_element_type.67, (f32[768,768]{1,0:T(8,128)}, f32[9,768]{1,0:T(8,128)}, f32[5,768]{1,0:T(8,128)}) %tuple.101, (pred[]{:T(512)}, s32[]{:T(128)}, ...), branch_computations={%region_1.1_spmd, %region_2.16_spmd} | conditional | flops 625999872 | bytes 22551692 | solution.py:180
  81.0 1.3 dynamic-slice_convert_fusion
  82.3 1.2 slice_reduce_fusion.12
  83.6 0.4 multiply_add_fusion.1
  83.9 2.1 multiply_reduce_fusion
  86.0 1.9 multiply_reduce_fusion.5
  88.1 1.4 add.258
  89.6 1.4 add.257
  91.0 0.5 fusion.30
  91.5 4.1 %bitcast_add_fusion = f32[768,768]{1,0:T(8,128)} fusion(f32[768,768]{1,0:T(8,128)} %get-tuple-element.418, bf16[2,8,4,4,768]{4,1,3,2,0:T(8,128)(2,1)S(1)} %get-tuple-element.504, f32[2,8,4,4,768]{4,1,3,2,0:T(8,128)S(1)} %multiply_add_fusion.1, f32[768]{0:T(1024)S(1)} %get-tuple-element.471, f32[768]{0:T(1024)S(1)} %get-tuple-element.472, ...), kind=kOutput, calls=%fused_computation.25 | convolution fusion | flops 305332224 | bytes 5913600 | tf_op jit(solution)/shard_map/while/body/eval_jaxpr/cond/branch_1_fun/dot_general | solution.py:131
  95.6 1.3 collective-permute-start
  96.9 11.4 %collective-permute-done = bf16[2,8,4,4,768]{4,1,3,2,0:T(8,128)(2,1)S(1)} collective-permute-done((bf16[2,8,4,4,768]{4,1,3,2,0:T(8,128)(2,1)S(1)}, bf16[2,8,4,4,768]{4,1,3,2,0:T(8,128)(2,1)S(1)}, u32[]{:S(2)}, u32[]{:S(2)}) %collective-permute-start) | collective-permute-done | bytes 393248 | tf_op jit(solution)/shard_map/while/body/eval_jaxpr/ppermute | solution.py:14
  108.2 14.6 %conditional.2 = (bf16[2,8,4,4,768]{4,1,3,2,0:T(8,128)(2,1)S(1)}, f32[768,768]{1,0:T(8,128)}, f32[9,768]{1,0:T(8,128)}, f32[5,768]{1,0:T(8,128)}) conditional(s32[]{:T(128)} %convert_element_type.67, (f32[768,768]{1,0:T(8,128)}, f32[9,768]{1,0:T(8,128)}, f32[5,768]{1,0:T(8,128)}) %tuple.101, (pred[]{:T(512)}, s32[]{:T(128)}, ...), branch_computations={%region_1.1_spmd, %region_2.16_spmd} | conditional | flops 625999872 | bytes 22551692 | solution.py:180
  108.2 1.3 dynamic-slice_convert_fusion
  109.5 1.2 slice_reduce_fusion.12
  111.2 2.1 multiply_reduce_fusion
  113.2 1.9 multiply_reduce_fusion.5
  115.4 1.4 add.258
  116.8 1.4 add.257
  118.2 0.5 fusion.30
  118.7 4.1 %bitcast_add_fusion = f32[768,768]{1,0:T(8,128)} fusion(f32[768,768]{1,0:T(8,128)} %get-tuple-element.418, bf16[2,8,4,4,768]{4,1,3,2,0:T(8,128)(2,1)S(1)} %get-tuple-element.504, f32[2,8,4,4,768]{4,1,3,2,0:T(8,128)S(1)} %multiply_add_fusion.1, f32[768]{0:T(1024)S(1)} %get-tuple-element.471, f32[768]{0:T(1024)S(1)} %get-tuple-element.472, ...), kind=kOutput, calls=%fused_computation.25 | convolution fusion | flops 305332224 | bytes 5913600 | tf_op jit(solution)/shard_map/while/body/eval_jaxpr/cond/branch_1_fun/dot_general | solution.py:131
  122.8 1.3 collective-permute-start
  124.1 10.5 %collective-permute-done = bf16[2,8,4,4,768]{4,1,3,2,0:T(8,128)(2,1)S(1)} collective-permute-done((bf16[2,8,4,4,768]{4,1,3,2,0:T(8,128)(2,1)S(1)}, bf16[2,8,4,4,768]{4,1,3,2,0:T(8,128)(2,1)S(1)}, u32[]{:S(2)}, u32[]{:S(2)}) %collective-permute-start) | collective-permute-done | bytes 393248 | tf_op jit(solution)/shard_map/while/body/eval_jaxpr/ppermute | solution.py:14
  134.6 14.6 %conditional.2 = (bf16[2,8,4,4,768]{4,1,3,2,0:T(8,128)(2,1)S(1)}, f32[768,768]{1,0:T(8,128)}, f32[9,768]{1,0:T(8,128)}, f32[5,768]{1,0:T(8,128)}) conditional(s32[]{:T(128)} %convert_element_type.67, (f32[768,768]{1,0:T(8,128)}, f32[9,768]{1,0:T(8,128)}, f32[5,768]{1,0:T(8,128)}) %tuple.101, (pred[]{:T(512)}, s32[]{:T(128)}, ...), branch_computations={%region_1.1_spmd, %region_2.16_spmd} | conditional | flops 625999872 | bytes 22551692 | solution.py:180
  134.6 1.3 dynamic-slice_convert_fusion
  135.9 1.2 slice_reduce_fusion.12
  137.5 2.1 multiply_reduce_fusion
  139.6 1.9 multiply_reduce_fusion.5
  141.7 1.4 add.258
  143.1 1.4 add.257
  144.5 0.5 fusion.30
  145.0 4.1 %bitcast_add_fusion = f32[768,768]{1,0:T(8,128)} fusion(f32[768,768]{1,0:T(8,128)} %get-tuple-element.418, bf16[2,8,4,4,768]{4,1,3,2,0:T(8,128)(2,1)S(1)} %get-tuple-element.504, f32[2,8,4,4,768]{4,1,3,2,0:T(8,128)S(1)} %multiply_add_fusion.1, f32[768]{0:T(1024)S(1)} %get-tuple-element.471, f32[768]{0:T(1024)S(1)} %get-tuple-element.472, ...), kind=kOutput, calls=%fused_computation.25 | convolution fusion | flops 305332224 | bytes 5913600 | tf_op jit(solution)/shard_map/while/body/eval_jaxpr/cond/branch_1_fun/dot_general | solution.py:131
  149.1 1.3 collective-permute-start
  150.4 9.6 %collective-permute-done = bf16[2,8,4,4,768]{4,1,3,2,0:T(8,128)(2,1)S(1)} collective-permute-done((bf16[2,8,4,4,768]{4,1,3,2,0:T(8,128)(2,1)S(1)}, bf16[2,8,4,4,768]{4,1,3,2,0:T(8,128)(2,1)S(1)}, u32[]{:S(2)}, u32[]{:S(2)}) %collective-permute-start) | collective-permute-done | bytes 393248 | tf_op jit(solution)/shard_map/while/body/eval_jaxpr/ppermute | solution.py:14
  160.0 14.6 %conditional.2 = (bf16[2,8,4,4,768]{4,1,3,2,0:T(8,128)(2,1)S(1)}, f32[768,768]{1,0:T(8,128)}, f32[9,768]{1,0:T(8,128)}, f32[5,768]{1,0:T(8,128)}) conditional(s32[]{:T(128)} %convert_element_type.67, (f32[768,768]{1,0:T(8,128)}, f32[9,768]{1,0:T(8,128)}, f32[5,768]{1,0:T(8,128)}) %tuple.101, (pred[]{:T(512)}, s32[]{:T(128)}, ...), branch_computations={%region_1.1_spmd, %region_2.16_spmd} | conditional | flops 625999872 | bytes 22551692 | solution.py:180
  160.0 1.3 dynamic-slice_convert_fusion
  161.3 1.2 slice_reduce_fusion.12
  162.5 0.4 multiply_add_fusion.1
  162.9 2.1 multiply_reduce_fusion
  165.0 1.9 multiply_reduce_fusion.5
  167.1 1.4 add.258
  168.5 1.4 add.257
  169.9 0.5 fusion.30
  170.4 4.1 %bitcast_add_fusion = f32[768,768]{1,0:T(8,128)} fusion(f32[768,768]{1,0:T(8,128)} %get-tuple-element.418, bf16[2,8,4,4,768]{4,1,3,2,0:T(8,128)(2,1)S(1)} %get-tuple-element.504, f32[2,8,4,4,768]{4,1,3,2,0:T(8,128)S(1)} %multiply_add_fusion.1, f32[768]{0:T(1024)S(1)} %get-tuple-element.471, f32[768]{0:T(1024)S(1)} %get-tuple-element.472, ...), kind=kOutput, calls=%fused_computation.25 | convolution fusion | flops 305332224 | bytes 5913600 | tf_op jit(solution)/shard_map/while/body/eval_jaxpr/cond/branch_1_fun/dot_general | solution.py:131
  174.5 1.3 collective-permute-start
  175.8 8.6 %collective-permute-done = bf16[2,8,4,4,768]{4,1,3,2,0:T(8,128)(2,1)S(1)} collective-permute-done((bf16[2,8,4,4,768]{4,1,3,2,0:T(8,128)(2,1)S(1)}, bf16[2,8,4,4,768]{4,1,3,2,0:T(8,128)(2,1)S(1)}, u32[]{:S(2)}, u32[]{:S(2)}) %collective-permute-start) | collective-permute-done | bytes 393248 | tf_op jit(solution)/shard_map/while/body/eval_jaxpr/ppermute | solution.py:14
  184.5 59.6 %all-reduce.4 = (f32[9,768]{1,0:T(8,128)S(1)}, f32[5,768]{1,0:T(8,128)S(1)}) all-reduce(f32[9,768]{1,0:T(8,128)} %get-tuple-element.445, f32[5,768]{1,0:T(8,128)} %get-tuple-element.446), channel_id=1, replica_groups=mesh['dp'=16,'section'=2] {'dp'}, use_global_device_ids=true, to_apply=%region_19.20 | all-reduce | flops 10752 | bytes 86016 | tf_op jit(solution)/shard_map/psum | solution.py:194
  244.1 0.6 broadcast_in_dim.37
  244.8 0.6 broadcast_in_dim.38
  245.4 0.7 reduce-scatter.2.cloned.1.call-done
  246.1 1.6 multiply_bitcast_fusion
  (91 shorter events, 1.9 us)
Async XLA Ops:
  7.2 6.6 %copy-start = (bf16[4,128,768]{2,1,0:T(8,128)(2,1)S(1)}, bf16[4,128,768]{2,1,0:T(8,128)(2,1)}, u32[]{:S(2)}) copy-start(bf16[4,128,768]{2,1,0:T(8,128)(2,1)} %param.17) | copy-start | bytes 2359300
  7.2 44.2 %all-gather.3.cloned.1.call-start = ((), (), s32[]{:S(2)}) async-start(), calls=%async_computation.2 | async-start | bytes 1253376 | tf_op jit(solution)/shard_map/all_gather | solution.py:155
  7.9 238.1 %reduce-scatter.2.cloned.1.call-start = ((), (), s32[]{:S(2)}) async-start(), calls=%async_computation.1 | async-start | bytes 2506752 | tf_op jit(solution)/shard_map/reduce_scatter | solution.py:193
  10.7 3.1 %copy-start.3 = (s32[8]{0:T(128)S(1)}, s32[8]{0:T(128)}, u32[]{:S(2)}) copy-start(s32[8]{0:T(128)} %param.13) | copy-start | bytes 100
  13.8 1.0 copy-start.2
  54.2 26.8 %collective-permute-start = (bf16[2,8,4,4,768]{4,1,3,2,0:T(8,128)(2,1)S(1)}, bf16[2,8,4,4,768]{4,1,3,2,0:T(8,128)(2,1)S(1)}, u32[]{:S(2)}, u32[]{:S(2)}) collective-permute-start(bf16[2,8,4,4,768]{4,1,3,2,0:T(8,128)(2,1)S(1)} %get-tuple-element.591), channel_id=1, source_target_pairs={{1,0},{3,2},{5,4},{7,6},{9,8},{11,10},{13,12},{15,14},{17,16},{19,... | collective-permute-start | bytes 1179656 | tf_op jit(solution)/shard_map/while/body/eval_jaxpr/ppermute | solution.py:14
  81.0 2.9 %copy-start.1 = (bf16[768,768]{1,0:T(8,128)(2,1)S(1)}, bf16[768,768]{1,0:T(8,128)(2,1)}, u32[]{:S(2)}) copy-start(bf16[768,768]{1,0:T(8,128)(2,1)} %get-tuple-element.416) | copy-start | bytes 3538948 | tf_op jit(solution)/shard_map/while/body/eval_jaxpr/cond
  95.6 12.7 %collective-permute-start = (bf16[2,8,4,4,768]{4,1,3,2,0:T(8,128)(2,1)S(1)}, bf16[2,8,4,4,768]{4,1,3,2,0:T(8,128)(2,1)S(1)}, u32[]{:S(2)}, u32[]{:S(2)}) collective-permute-start(bf16[2,8,4,4,768]{4,1,3,2,0:T(8,128)(2,1)S(1)} %get-tuple-element.591), channel_id=1, source_target_pairs={{1,0},{3,2},{5,4},{7,6},{9,8},{11,10},{13,12},{15,14},{17,16},{19,... | collective-permute-start | bytes 1179656 | tf_op jit(solution)/shard_map/while/body/eval_jaxpr/ppermute | solution.py:14
  108.2 2.9 %copy-start.1 = (bf16[768,768]{1,0:T(8,128)(2,1)S(1)}, bf16[768,768]{1,0:T(8,128)(2,1)}, u32[]{:S(2)}) copy-start(bf16[768,768]{1,0:T(8,128)(2,1)} %get-tuple-element.416) | copy-start | bytes 3538948 | tf_op jit(solution)/shard_map/while/body/eval_jaxpr/cond
  122.8 11.8 %collective-permute-start = (bf16[2,8,4,4,768]{4,1,3,2,0:T(8,128)(2,1)S(1)}, bf16[2,8,4,4,768]{4,1,3,2,0:T(8,128)(2,1)S(1)}, u32[]{:S(2)}, u32[]{:S(2)}) collective-permute-start(bf16[2,8,4,4,768]{4,1,3,2,0:T(8,128)(2,1)S(1)} %get-tuple-element.591), channel_id=1, source_target_pairs={{1,0},{3,2},{5,4},{7,6},{9,8},{11,10},{13,12},{15,14},{17,16},{19,... | collective-permute-start | bytes 1179656 | tf_op jit(solution)/shard_map/while/body/eval_jaxpr/ppermute | solution.py:14
  134.6 2.9 %copy-start.1 = (bf16[768,768]{1,0:T(8,128)(2,1)S(1)}, bf16[768,768]{1,0:T(8,128)(2,1)}, u32[]{:S(2)}) copy-start(bf16[768,768]{1,0:T(8,128)(2,1)} %get-tuple-element.416) | copy-start | bytes 3538948 | tf_op jit(solution)/shard_map/while/body/eval_jaxpr/cond
  149.1 10.9 %collective-permute-start = (bf16[2,8,4,4,768]{4,1,3,2,0:T(8,128)(2,1)S(1)}, bf16[2,8,4,4,768]{4,1,3,2,0:T(8,128)(2,1)S(1)}, u32[]{:S(2)}, u32[]{:S(2)}) collective-permute-start(bf16[2,8,4,4,768]{4,1,3,2,0:T(8,128)(2,1)S(1)} %get-tuple-element.591), channel_id=1, source_target_pairs={{1,0},{3,2},{5,4},{7,6},{9,8},{11,10},{13,12},{15,14},{17,16},{19,... | collective-permute-start | bytes 1179656 | tf_op jit(solution)/shard_map/while/body/eval_jaxpr/ppermute | solution.py:14
  160.0 2.9 %copy-start.1 = (bf16[768,768]{1,0:T(8,128)(2,1)S(1)}, bf16[768,768]{1,0:T(8,128)(2,1)}, u32[]{:S(2)}) copy-start(bf16[768,768]{1,0:T(8,128)(2,1)} %get-tuple-element.416) | copy-start | bytes 3538948 | tf_op jit(solution)/shard_map/while/body/eval_jaxpr/cond
  174.5 9.9 %collective-permute-start = (bf16[2,8,4,4,768]{4,1,3,2,0:T(8,128)(2,1)S(1)}, bf16[2,8,4,4,768]{4,1,3,2,0:T(8,128)(2,1)S(1)}, u32[]{:S(2)}, u32[]{:S(2)}) collective-permute-start(bf16[2,8,4,4,768]{4,1,3,2,0:T(8,128)(2,1)S(1)} %get-tuple-element.591), channel_id=1, source_target_pairs={{1,0},{3,2},{5,4},{7,6},{9,8},{11,10},{13,12},{15,14},{17,16},{19,... | collective-permute-start | bytes 1179656 | tf_op jit(solution)/shard_map/while/body/eval_jaxpr/ppermute | solution.py:14
Sparse Core Ops, SparseCore 0:
  10.3 41.0 all-gather.2
  184.6 61.4 reduce-scatter.1
where the time goes:
time: 256 us; the launch traced here: 254 us
  waiting for transfers between devices  102 us (40%)
  blocking collectives  59.6 us (23%)
  other arithmetic  28.9 us (11%)
  matrix products  26.5 us (10%)
  local copies, waits for them, and re-layouts  16.4 us (6%)
  between operations  14.1 us (6%)
  starting transfers between devices  6.49 us (3%)
    ppermute x5, waiting for transfers between devices, from_behind(): return lax.ppermute(block, axis, route)  65.5 us
    psum x1, blocking collectives, local(): s_total, t_total = lax.psum((finals[2], finals[3]), 'dp')  59.6 us
    all_gather x1, waiting for transfers between devices, local(): full_weight = lax.all_gather(weight_shard, 'dp', axis=0, tiled=True)  34.8 us
    dot_general x4, matrix products, section_back(): jnp.dot(flat_hidden.T, flat_grad, preferred_element_type=jnp.float32)  16.4 us
    add x8, other arithmetic, live_work(): return (in_grad, sums[0] + w_part, sums[1] + s_part, sums[2] + t_part)  11.1 us
    dot_general x4, matrix products, hidden_of(): return jnp.dot(flat_grad, full_weight.T, preferred_element_type=jnp.float32)  8.29 us
    reduce_sum x4, other arithmetic, spatial_kernel_grad(): jnp.sum(padded[..., row_off:row_off + height, col_off:col_off + width, :]...  7.66 us
    ppermute x5, starting transfers between devices, from_behind(): return lax.ppermute(block, axis, route)  6.41 us
  transfers between devices with their start and end apart: 7, of which 7 were waited for; matrix products, arithmetic and copies ran while one was open for 4% of the time, Pallas kernels for 0%

commit v1 on v0

--- a/solution.py
+++ b/solution.py
@@ -152,7 +152,14 @@
     block_size = 2
     step_count = clip_count // block_size
     tick_count = step_count + section_count - 1
-    full_weight = lax.all_gather(weight_shard, "dp", axis=0, tiled=True)
+    ways, here = (lax.axis_size("dp"), lax.axis_index("dp"))
+    full_weight, reach = (weight_shard, 1)
+    while reach < ways:
+        theirs = lax.ppermute(full_weight, "dp", [(d, d ^ reach) for d in range(ways)])
+        mine_first = jnp.concatenate([full_weight, theirs], axis=0)
+        theirs_first = jnp.concatenate([theirs, full_weight], axis=0)
+        full_weight = jnp.where(here & reach == 0, mine_first, theirs_first)
+        reach = 2 * reach
 
     def hidden_of(flat_grad):
         return jnp.dot(flat_grad, full_weight.T, preferred_element_type=jnp.float32)

time: 256 us -> 261 us (1.020)
  waiting for transfers between devices: 102 us -> 93.5 us
  starting transfers between devices: 6.49 us -> 14.2 us
  blocking collectives: 59.6 us -> 63 us
  other arithmetic: 28.9 us -> 31.7 us
    all_gather x1 -> x0, waiting for transfers between devices: 34.8 us -> none  [local(): full_weight = lax.all_gather(weight_shard, 'dp', axis=0, tiled=True)]
    ppermute x0 -> x4, waiting for transfers between devices: none -> 31 us  [local(): lax.ppermute(full_weight, 'dp', [(d, d ^ reach) for d in range(ways)])]
    ppermute x0 -> x4, starting transfers between devices: none -> 7.72 us  [local(): lax.ppermute(full_weight, 'dp', [(d, d ^ reach) for d in range(ways)])]
    ppermute x5, waiting for transfers between devices: 65.5 us -> 59.8 us  [from_behind(): return lax.ppermute(block, axis, route)]
    psum x1, blocking collectives: 59.6 us -> 63 us  [local(): s_total, t_total = lax.psum((finals[2], finals[3]), 'dp')]
    select_n x0 -> x4, other arithmetic: none -> 2.72 us  [local(): full_weight = jnp.where(here & reach == 0, mine_first, theirs_first)]
  transfers between devices with their start and end apart: 7 -> 10, of which waited for: 7 -> 9; matrix products, arithmetic and copies ran while one was open for 4% -> 4% of each run, Pallas kernels for 0% -> 0%
where the time goes in v1:
time: 261 us; the launch traced here: 260 us
  waiting for transfers between devices  93.5 us (36%)
  blocking collectives  63 us (24%)
  other arithmetic  31.7 us (12%)
  matrix products  26.5 us (10%)
  local copies, waits for them, and re-layouts  16.2 us (6%)
  starting transfers between devices  14.2 us (5%)
  between operations  14.1 us (5%)
    psum x1, blocking collectives, local(): s_total, t_total = lax.psum((finals[2], finals[3]), 'dp')  63 us
    ppermute x5, waiting for transfers between devices, from_behind(): return lax.ppermute(block, axis, route)  59.8 us
    ppermute x4, waiting for transfers between devices, local(): lax.ppermute(full_weight, 'dp', [(d, d ^ reach) for d in range(ways)])  31 us
    dot_general x4, matrix products, section_back(): jnp.dot(flat_hidden.T, flat_grad, preferred_element_type=jnp.float32)  16.4 us
    add x8, other arithmetic, live_work(): return (in_grad, sums[0] + w_part, sums[1] + s_part, sums[2] + t_part)  11.1 us
    dot_general x4, matrix products, hidden_of(): return jnp.dot(flat_grad, full_weight.T, preferred_element_type=jnp.float32)  8.3 us
    ppermute x4, starting transfers between devices, local(): lax.ppermute(full_weight, 'dp', [(d, d ^ reach) for d in range(ways)])  7.72 us
    reduce_sum x4, other arithmetic, spatial_kernel_grad(): jnp.sum(padded[..., row_off:row_off + height, col_off:col_off + width, :]...  7.66 us
  transfers between devices with their start and end apart: 10, of which 9 were waited for; matrix products, arithmetic and copies ran while one was open for 4% of the time, Pallas kernels for 0%

profile of v1, /device:TPU:0, one launch (start us, length us, event | category | flops | bytes accessed | tf_op | source)
XLA Modules:
  0.0 259.8 jit_solution(4412056679863201709)
XLA Ops:
  7.7 1.1 collective-permute-done.1
  8.9 1.0 maximum_select_fusion.3
  9.9 2.9 %collective-permute-start.2 = (bf16[96,768]{1,0:T(8,128)(2,1)S(1)}, bf16[96,768]{1,0:T(8,128)(2,1)S(1)}, u32[]{:S(2)}, u32[]{:S(2)}) collective-permute-start(bf16[96,768]{1,0:T(8,128)(2,1)S(1)} %maximum_select_fusion.3), channel_id=1, source_target_pairs={{0,4},{2,6},{4,0},{6,2},{8,12},{10,14},{12,8},{14,10},{16,20},{18,... | collective-permute-start | bytes 442376 | tf_op jit(solution)/shard_map/ppermute | solution.py:158
  12.8 1.3 copy.24
  14.1 1.4 copy.23
  15.5 3.1 %copy.22 = bf16[1,8,8,4,4,768]{5,2,4,3,1,0:T(8,128)(2,1)} copy(bf16[1,8,8,4,4,768]{5,4,3,2,1,0:T(4,128)(2,1)} %param.11) | data formatting | bytes 3145728 | tf_op args[0]
  18.6 1.6 collective-permute-start.3
  20.3 0.6 gather_fusion
  20.9 6.5 %collective-permute-done.3 = bf16[192,768]{1,0:T(8,128)(2,1)S(1)} collective-permute-done((bf16[192,768]{1,0:T(8,128)(2,1)S(1)}, bf16[192,768]{1,0:T(8,128)(2,1)S(1)}, u32[]{:S(2)}, u32[]{:S(2)}) %collective-permute-start.3) | collective-permute-done | bytes 294944 | tf_op jit(solution)/shard_map/ppermute | solution.py:158
  27.7 2.7 %collective-permute-start.4 = (bf16[384,768]{1,0:T(8,128)(2,1)S(1)}, bf16[384,768]{1,0:T(8,128)(2,1)S(1)}, u32[]{:S(2)}, u32[]{:S(2)}) collective-permute-start(bf16[384,768]{1,0:T(8,128)(2,1)S(1)} %maximum_select_fusion.1), channel_id=1, source_target_pairs={{0,16},{2,18},{4,20},{6,22},{8,24},{10,26},{12,28},{14,30},{16,0},... | collective-permute-start | bytes 1769480 | tf_op jit(solution)/shard_map/ppermute | solution.py:158
  30.3 1.8 fusion.36
  32.1 23.4 %collective-permute-done.4 = bf16[384,768]{1,0:T(8,128)(2,1)S(1)} collective-permute-done((bf16[384,768]{1,0:T(8,128)(2,1)S(1)}, bf16[384,768]{1,0:T(8,128)(2,1)S(1)}, u32[]{:S(2)}, u32[]{:S(2)}) %collective-permute-start.4) | collective-permute-done | bytes 589856 | tf_op jit(solution)/shard_map/ppermute | solution.py:158
  55.5 1.5 maximum_select_fusion
  57.0 0.6 broadcast_in_dim.32
  57.6 0.6 broadcast_in_dim.31
  58.3 1.6 broadcast_in_dim.30
  59.8 124.6 %while.21 = (s32[]{:T(128)}, bf16[2,8,4,4,768]{4,1,3,2,0:T(8,128)(2,1)S(1)}, f32[768,768]{1,0:T(8,128)}, f32[9,768]{1,0:T(8,128)}, f32[5,768]{1,0:T(8,128)}, /*i...) while((s32[]{:T(128)}, ...), condition=%wide.region_17.18_spmd, body=%wide.region_0.17_spmd.sunk | while | flops 625999872 | bytes 24124888 | solution.py:199
  59.9 1.3 collective-permute-start
  61.2 24.2 %collective-permute-done = bf16[2,8,4,4,768]{4,1,3,2,0:T(8,128)(2,1)S(1)} collective-permute-done((bf16[2,8,4,4,768]{4,1,3,2,0:T(8,128)(2,1)S(1)}, bf16[2,8,4,4,768]{4,1,3,2,0:T(8,128)(2,1)S(1)}, u32[]{:S(2)}, u32[]{:S(2)}) %collective-permute-start) | collective-permute-done | bytes 393248 | tf_op jit(solution)/shard_map/while/body/eval_jaxpr/ppermute | solution.py:14
  85.4 14.6 %conditional.2 = (bf16[2,8,4,4,768]{4,1,3,2,0:T(8,128)(2,1)S(1)}, f32[768,768]{1,0:T(8,128)}, f32[9,768]{1,0:T(8,128)}, f32[5,768]{1,0:T(8,128)}) conditional(s32[]{:T(128)} %convert_element_type.67, (f32[768,768]{1,0:T(8,128)}, f32[9,768]{1,0:T(8,128)}, f32[5,768]{1,0:T(8,128)}) %tuple.101, (pred[]{:T(512)}, s32[]{:T(128)}, ...), branch_computations={%region_1.1_spmd, %region_2.16_spmd} | conditional | flops 625999872 | bytes 22551692 | solution.py:187
  85.4 1.3 dynamic-slice_convert_fusion
  86.7 1.2 slice_reduce_fusion.12
  88.3 2.1 multiply_reduce_fusion
  90.4 1.9 multiply_reduce_fusion.5
  92.5 1.4 add.258
  93.9 1.4 add.257
  95.8 4.1 %bitcast_add_fusion = f32[768,768]{1,0:T(8,128)} fusion(f32[768,768]{1,0:T(8,128)} %get-tuple-element.418, bf16[2,8,4,4,768]{4,1,3,2,0:T(8,128)(2,1)S(1)} %get-tuple-element.504, f32[2,8,4,4,768]{4,1,3,2,0:T(8,128)S(1)} %multiply_add_fusion.1, f32[768]{0:T(1024)S(1)} %get-tuple-element.471, f32[768]{0:T(1024)S(1)} %get-tuple-element.472, ...), kind=kOutput, calls=%fused_computation.25 | convolution fusion | flops 305332224 | bytes 5913600 | tf_op jit(solution)/shard_map/while/body/eval_jaxpr/cond/branch_1_fun/dot_general | solution.py:131
  99.9 1.3 collective-permute-start
  101.2 9.9 %collective-permute-done = bf16[2,8,4,4,768]{4,1,3,2,0:T(8,128)(2,1)S(1)} collective-permute-done((bf16[2,8,4,4,768]{4,1,3,2,0:T(8,128)(2,1)S(1)}, bf16[2,8,4,4,768]{4,1,3,2,0:T(8,128)(2,1)S(1)}, u32[]{:S(2)}, u32[]{:S(2)}) %collective-permute-start) | collective-permute-done | bytes 393248 | tf_op jit(solution)/shard_map/while/body/eval_jaxpr/ppermute | solution.py:14
  111.1 14.6 %conditional.2 = (bf16[2,8,4,4,768]{4,1,3,2,0:T(8,128)(2,1)S(1)}, f32[768,768]{1,0:T(8,128)}, f32[9,768]{1,0:T(8,128)}, f32[5,768]{1,0:T(8,128)}) conditional(s32[]{:T(128)} %convert_element_type.67, (f32[768,768]{1,0:T(8,128)}, f32[9,768]{1,0:T(8,128)}, f32[5,768]{1,0:T(8,128)}) %tuple.101, (pred[]{:T(512)}, s32[]{:T(128)}, ...), branch_computations={%region_1.1_spmd, %region_2.16_spmd} | conditional | flops 625999872 | bytes 22551692 | solution.py:187
  111.1 1.3 dynamic-slice_convert_fusion
  112.4 1.2 slice_reduce_fusion.12
  114.1 2.1 multiply_reduce_fusion
  116.2 1.9 multiply_reduce_fusion.5
  118.3 1.4 add.258
  119.7 1.4 add.257
  121.6 4.1 %bitcast_add_fusion = f32[768,768]{1,0:T(8,128)} fusion(f32[768,768]{1,0:T(8,128)} %get-tuple-element.418, bf16[2,8,4,4,768]{4,1,3,2,0:T(8,128)(2,1)S(1)} %get-tuple-element.504, f32[2,8,4,4,768]{4,1,3,2,0:T(8,128)S(1)} %multiply_add_fusion.1, f32[768]{0:T(1024)S(1)} %get-tuple-element.471, f32[768]{0:T(1024)S(1)} %get-tuple-element.472, ...), kind=kOutput, calls=%fused_computation.25 | convolution fusion | flops 305332224 | bytes 5913600 | tf_op jit(solution)/shard_map/while/body/eval_jaxpr/cond/branch_1_fun/dot_general | solution.py:131
  125.7 1.3 collective-permute-start
  127.0 9.0 %collective-permute-done = bf16[2,8,4,4,768]{4,1,3,2,0:T(8,128)(2,1)S(1)} collective-permute-done((bf16[2,8,4,4,768]{4,1,3,2,0:T(8,128)(2,1)S(1)}, bf16[2,8,4,4,768]{4,1,3,2,0:T(8,128)(2,1)S(1)}, u32[]{:S(2)}, u32[]{:S(2)}) %collective-permute-start) | collective-permute-done | bytes 393248 | tf_op jit(solution)/shard_map/while/body/eval_jaxpr/ppermute | solution.py:14
  136.0 14.6 %conditional.2 = (bf16[2,8,4,4,768]{4,1,3,2,0:T(8,128)(2,1)S(1)}, f32[768,768]{1,0:T(8,128)}, f32[9,768]{1,0:T(8,128)}, f32[5,768]{1,0:T(8,128)}) conditional(s32[]{:T(128)} %convert_element_type.67, (f32[768,768]{1,0:T(8,128)}, f32[9,768]{1,0:T(8,128)}, f32[5,768]{1,0:T(8,128)}) %tuple.101, (pred[]{:T(512)}, s32[]{:T(128)}, ...), branch_computations={%region_1.1_spmd, %region_2.16_spmd} | conditional | flops 625999872 | bytes 22551692 | solution.py:187
  136.0 1.3 dynamic-slice_convert_fusion
  137.3 1.2 slice_reduce_fusion.12
  138.9 2.1 multiply_reduce_fusion
  141.0 1.9 multiply_reduce_fusion.5
  143.1 1.4 add.258
  144.5 1.4 add.257
  146.4 4.1 %bitcast_add_fusion = f32[768,768]{1,0:T(8,128)} fusion(f32[768,768]{1,0:T(8,128)} %get-tuple-element.418, bf16[2,8,4,4,768]{4,1,3,2,0:T(8,128)(2,1)S(1)} %get-tuple-element.504, f32[2,8,4,4,768]{4,1,3,2,0:T(8,128)S(1)} %multiply_add_fusion.1, f32[768]{0:T(1024)S(1)} %get-tuple-element.471, f32[768]{0:T(1024)S(1)} %get-tuple-element.472, ...), kind=kOutput, calls=%fused_computation.25 | convolution fusion | flops 305332224 | bytes 5913600 | tf_op jit(solution)/shard_map/while/body/eval_jaxpr/cond/branch_1_fun/dot_general | solution.py:131
  150.5 1.3 collective-permute-start
  151.8 8.4 %collective-permute-done = bf16[2,8,4,4,768]{4,1,3,2,0:T(8,128)(2,1)S(1)} collective-permute-done((bf16[2,8,4,4,768]{4,1,3,2,0:T(8,128)(2,1)S(1)}, bf16[2,8,4,4,768]{4,1,3,2,0:T(8,128)(2,1)S(1)}, u32[]{:S(2)}, u32[]{:S(2)}) %collective-permute-start) | collective-permute-done | bytes 393248 | tf_op jit(solution)/shard_map/while/body/eval_jaxpr/ppermute | solution.py:14
  160.2 14.6 %conditional.2 = (bf16[2,8,4,4,768]{4,1,3,2,0:T(8,128)(2,1)S(1)}, f32[768,768]{1,0:T(8,128)}, f32[9,768]{1,0:T(8,128)}, f32[5,768]{1,0:T(8,128)}) conditional(s32[]{:T(128)} %convert_element_type.67, (f32[768,768]{1,0:T(8,128)}, f32[9,768]{1,0:T(8,128)}, f32[5,768]{1,0:T(8,128)}) %tuple.101, (pred[]{:T(512)}, s32[]{:T(128)}, ...), branch_computations={%region_1.1_spmd, %region_2.16_spmd} | conditional | flops 625999872 | bytes 22551692 | solution.py:187
  160.2 1.3 dynamic-slice_convert_fusion
  161.5 1.2 slice_reduce_fusion.12
  163.1 2.1 multiply_reduce_fusion
  165.2 1.9 multiply_reduce_fusion.5
  167.3 1.4 add.258
  168.7 1.4 add.257
  170.7 4.1 %bitcast_add_fusion = f32[768,768]{1,0:T(8,128)} fusion(f32[768,768]{1,0:T(8,128)} %get-tuple-element.418, bf16[2,8,4,4,768]{4,1,3,2,0:T(8,128)(2,1)S(1)} %get-tuple-element.504, f32[2,8,4,4,768]{4,1,3,2,0:T(8,128)S(1)} %multiply_add_fusion.1, f32[768]{0:T(1024)S(1)} %get-tuple-element.471, f32[768]{0:T(1024)S(1)} %get-tuple-element.472, ...), kind=kOutput, calls=%fused_computation.25 | convolution fusion | flops 305332224 | bytes 5913600 | tf_op jit(solution)/shard_map/while/body/eval_jaxpr/cond/branch_1_fun/dot_general | solution.py:131
  174.8 1.3 collective-permute-start
  176.0 8.4 %collective-permute-done = bf16[2,8,4,4,768]{4,1,3,2,0:T(8,128)(2,1)S(1)} collective-permute-done((bf16[2,8,4,4,768]{4,1,3,2,0:T(8,128)(2,1)S(1)}, bf16[2,8,4,4,768]{4,1,3,2,0:T(8,128)(2,1)S(1)}, u32[]{:S(2)}, u32[]{:S(2)}) %collective-permute-start) | collective-permute-done | bytes 393248 | tf_op jit(solution)/shard_map/while/body/eval_jaxpr/ppermute | solution.py:14
  184.4 63.0 %all-reduce.4 = (f32[9,768]{1,0:T(8,128)S(1)}, f32[5,768]{1,0:T(8,128)S(1)}) all-reduce(f32[9,768]{1,0:T(8,128)} %get-tuple-element.445, f32[5,768]{1,0:T(8,128)} %get-tuple-element.446), channel_id=1, replica_groups=mesh['dp'=16,'section'=2] {'dp'}, use_global_device_ids=true, to_apply=%region_19.20 | all-reduce | flops 10752 | bytes 86016 | tf_op jit(solution)/shard_map/psum | solution.py:201
  247.4 0.6 broadcast_in_dim.37
  248.0 0.6 broadcast_in_dim.38
  248.7 2.7 %reduce-scatter.2.cloned.1.call-done = f32[48,768]{1,0:T(8,128)} async-done(((f32[768,768]{1,0:T(8,128)}), f32[48,768]{1,0:T(8,128)}) %reduce-scatter.2.cloned.1.call-update) | async-done | bytes 147472 | tf_op jit(solution)/shard_map/reduce_scatter | solution.py:200
  251.3 1.6 multiply_bitcast_fusion
  (100 shorter events, 5.0 us)
Async XLA Ops:
  7.2 13.1 %copy-start = (bf16[4,128,768]{2,1,0:T(8,128)(2,1)S(1)}, bf16[4,128,768]{2,1,0:T(8,128)(2,1)}, u32[]{:S(2)}) copy-start(bf16[4,128,768]{2,1,0:T(8,128)(2,1)} %param.17) | copy-start | bytes 2359300
  7.2 244.1 %reduce-scatter.2.cloned.1.call-start = ((), (), s32[]{:S(2)}) async-start(), calls=%async_computation.1 | async-start | bytes 2506752 | tf_op jit(solution)/shard_map/reduce_scatter | solution.py:200
  7.2 1.6 collective-permute-start.1
  9.9 8.7 %collective-permute-start.2 = (bf16[96,768]{1,0:T(8,128)(2,1)S(1)}, bf16[96,768]{1,0:T(8,128)(2,1)S(1)}, u32[]{:S(2)}, u32[]{:S(2)}) collective-permute-start(bf16[96,768]{1,0:T(8,128)(2,1)S(1)} %maximum_select_fusion.3), channel_id=1, source_target_pairs={{0,4},{2,6},{4,0},{6,2},{8,12},{10,14},{12,8},{14,10},{16,20},{18,... | collective-permute-start | bytes 442376 | tf_op jit(solution)/shard_map/ppermute | solution.py:158
  15.5 4.8 %copy-start.3 = (s32[8]{0:T(128)S(1)}, s32[8]{0:T(128)}, u32[]{:S(2)}) copy-start(s32[8]{0:T(128)} %param.13) | copy-start | bytes 100
  18.6 8.9 %collective-permute-start.3 = (bf16[192,768]{1,0:T(8,128)(2,1)S(1)}, bf16[192,768]{1,0:T(8,128)(2,1)S(1)}, u32[]{:S(2)}, u32[]{:S(2)}) collective-permute-start(bf16[192,768]{1,0:T(8,128)(2,1)S(1)} %maximum_select_fusion.2), channel_id=1, source_target_pairs={{0,8},{2,10},{4,12},{6,14},{8,0},{10,2},{12,4},{14,6},{16,24},{18,... | collective-permute-start | bytes 884744 | tf_op jit(solution)/shard_map/ppermute | solution.py:158
  20.3 10.0 %copy-start.2 = (bf16[8,8,4,4,128]{4,3,2,1,0:T(4,128)(2,1)S(1)}, bf16[8,8,4,4,128]{4,3,2,1,0:T(4,128)(2,1)}, u32[]{:S(2)}) copy-start(bf16[8,8,4,4,128]{4,3,2,1,0:T(4,128)(2,1)} %param.12) | copy-start | bytes 786436
  27.7 27.8 %collective-permute-start.4 = (bf16[384,768]{1,0:T(8,128)(2,1)S(1)}, bf16[384,768]{1,0:T(8,128)(2,1)S(1)}, u32[]{:S(2)}, u32[]{:S(2)}) collective-permute-start(bf16[384,768]{1,0:T(8,128)(2,1)S(1)} %maximum_select_fusion.1), channel_id=1, source_target_pairs={{0,16},{2,18},{4,20},{6,22},{8,24},{10,26},{12,28},{14,30},{16,0},... | collective-permute-start | bytes 1769480 | tf_op jit(solution)/shard_map/ppermute | solution.py:158
  59.9 25.5 %collective-permute-start = (bf16[2,8,4,4,768]{4,1,3,2,0:T(8,128)(2,1)S(1)}, bf16[2,8,4,4,768]{4,1,3,2,0:T(8,128)(2,1)S(1)}, u32[]{:S(2)}, u32[]{:S(2)}) collective-permute-start(bf16[2,8,4,4,768]{4,1,3,2,0:T(8,128)(2,1)S(1)} %get-tuple-element.591), channel_id=1, source_target_pairs={{1,0},{3,2},{5,4},{7,6},{9,8},{11,10},{13,12},{15,14},{17,16},{19,... | collective-permute-start | bytes 1179656 | tf_op jit(solution)/shard_map/while/body/eval_jaxpr/ppermute | solution.py:14
  85.4 2.9 %copy-start.1 = (bf16[768,768]{1,0:T(8,128)(2,1)S(1)}, bf16[768,768]{1,0:T(8,128)(2,1)}, u32[]{:S(2)}) copy-start(bf16[768,768]{1,0:T(8,128)(2,1)} %get-tuple-element.416) | copy-start | bytes 3538948 | tf_op jit(solution)/shard_map/while/body/eval_jaxpr/cond
  99.9 11.2 %collective-permute-start = (bf16[2,8,4,4,768]{4,1,3,2,0:T(8,128)(2,1)S(1)}, bf16[2,8,4,4,768]{4,1,3,2,0:T(8,128)(2,1)S(1)}, u32[]{:S(2)}, u32[]{:S(2)}) collective-permute-start(bf16[2,8,4,4,768]{4,1,3,2,0:T(8,128)(2,1)S(1)} %get-tuple-element.591), channel_id=1, source_target_pairs={{1,0},{3,2},{5,4},{7,6},{9,8},{11,10},{13,12},{15,14},{17,16},{19,... | collective-permute-start | bytes 1179656 | tf_op jit(solution)/shard_map/while/body/eval_jaxpr/ppermute | solution.py:14
  111.1 2.9 %copy-start.1 = (bf16[768,768]{1,0:T(8,128)(2,1)S(1)}, bf16[768,768]{1,0:T(8,128)(2,1)}, u32[]{:S(2)}) copy-start(bf16[768,768]{1,0:T(8,128)(2,1)} %get-tuple-element.416) | copy-start | bytes 3538948 | tf_op jit(solution)/shard_map/while/body/eval_jaxpr/cond
  125.7 10.3 %collective-permute-start = (bf16[2,8,4,4,768]{4,1,3,2,0:T(8,128)(2,1)S(1)}, bf16[2,8,4,4,768]{4,1,3,2,0:T(8,128)(2,1)S(1)}, u32[]{:S(2)}, u32[]{:S(2)}) collective-permute-start(bf16[2,8,4,4,768]{4,1,3,2,0:T(8,128)(2,1)S(1)} %get-tuple-element.591), channel_id=1, source_target_pairs={{1,0},{3,2},{5,4},{7,6},{9,8},{11,10},{13,12},{15,14},{17,16},{19,... | collective-permute-start | bytes 1179656 | tf_op jit(solution)/shard_map/while/body/eval_jaxpr/ppermute | solution.py:14
  136.0 2.9 %copy-start.1 = (bf16[768,768]{1,0:T(8,128)(2,1)S(1)}, bf16[768,768]{1,0:T(8,128)(2,1)}, u32[]{:S(2)}) copy-start(bf16[768,768]{1,0:T(8,128)(2,1)} %get-tuple-element.416) | copy-start | bytes 3538948 | tf_op jit(solution)/shard_map/while/body/eval_jaxpr/cond
  150.5 9.7 %collective-permute-start = (bf16[2,8,4,4,768]{4,1,3,2,0:T(8,128)(2,1)S(1)}, bf16[2,8,4,4,768]{4,1,3,2,0:T(8,128)(2,1)S(1)}, u32[]{:S(2)}, u32[]{:S(2)}) collective-permute-start(bf16[2,8,4,4,768]{4,1,3,2,0:T(8,128)(2,1)S(1)} %get-tuple-element.591), channel_id=1, source_target_pairs={{1,0},{3,2},{5,4},{7,6},{9,8},{11,10},{13,12},{15,14},{17,16},{19,... | collective-permute-start | bytes 1179656 | tf_op jit(solution)/shard_map/while/body/eval_jaxpr/ppermute | solution.py:14
  160.2 2.9 %copy-start.1 = (bf16[768,768]{1,0:T(8,128)(2,1)S(1)}, bf16[768,768]{1,0:T(8,128)(2,1)}, u32[]{:S(2)}) copy-start(bf16[768,768]{1,0:T(8,128)(2,1)} %get-tuple-element.416) | copy-start | bytes 3538948 | tf_op jit(solution)/shard_map/while/body/eval_jaxpr/cond
  174.8 9.7 %collective-permute-start = (bf16[2,8,4,4,768]{4,1,3,2,0:T(8,128)(2,1)S(1)}, bf16[2,8,4,4,768]{4,1,3,2,0:T(8,128)(2,1)S(1)}, u32[]{:S(2)}, u32[]{:S(2)}) collective-permute-start(bf16[2,8,4,4,768]{4,1,3,2,0:T(8,128)(2,1)S(1)} %get-tuple-element.591), channel_id=1, source_target_pairs={{1,0},{3,2},{5,4},{7,6},{9,8},{11,10},{13,12},{15,14},{17,16},{19,... | collective-permute-start | bytes 1179656 | tf_op jit(solution)/shard_map/while/body/eval_jaxpr/ppermute | solution.py:14
Sparse Core Ops, SparseCore 0:
  184.6 66.7 reduce-scatter.1
